TPU v7x, 32 devices: a whole 2x2x4 slice. The times are simulated.
32 devices in a mesh: chan: 16 (over z, y, core), band: 2 (over x).
Axes of the slice: x: 2, y: 2, z: 4, core: 2. Of those that a mesh axis runs over, the one named last changes fastest.
Arguments:
- strain: bfloat16 [4096, 4, 4096], P('chan', None, 'band'), may hold values from -6 to 6
- band_start: int32 [2], replicated, may hold values from 4 to 818
Outputs:
- coherency: bfloat16 [2, 2, 4096, 4096], P('band', None, 'chan')
All inputs are finite; a program needn't handle non-finite values.
Results may differ from a plain program's by a relative error of at most 0.0056.
Values may be sent and summed in bfloat16 or wider, within the bound.
A program may use at most 64 MiB of HBM per device.

v0:
```python
import math
import jax
import jax.numpy as jnp
from jax import lax
from jax.sharding import PartitionSpec as P

WINDOW_SAMPLES = 4096
K = 32


def dft_table(freqs, positions):
    phase_angles = positions[:, None, None] * freqs[None, :, :] % WINDOW_SAMPLES
    angles = phase_angles.astype(jnp.float32) * (2.0 * math.pi / WINDOW_SAMPLES)
    taper = 0.5 - 0.5 * jnp.cos(positions.astype(jnp.float32) * (2.0 * math.pi / WINDOW_SAMPLES))
    cosine = taper[:, None, None] * jnp.cos(angles)
    sine = -taper[:, None, None] * jnp.sin(angles)
    return jnp.concatenate([cosine, sine], axis=2).astype(jnp.bfloat16)


def whiten(spectrum, chans, windows):
    power = jnp.mean(spectrum * spectrum, axis=1, keepdims=True)
    whitened = (spectrum * lax.rsqrt(power + 1e-06)).astype(jnp.bfloat16)
    return (
        whitened.reshape(chans, windows, 2, K).transpose(0, 2, 1, 3).reshape(chans, 2 * windows * K)
    )


def cross_block(local_panel_rows, other_panel):
    half_feat = other_panel.shape[1] // 2
    rotated = jnp.concatenate([-other_panel[:, half_feat:], other_panel[:, :half_feat]], axis=1)
    stacked_spectra = jnp.stack([other_panel, rotated])
    cross_product = jnp.einsum(
        "gb,ozb->ogz", local_panel_rows, stacked_spectra, preferred_element_type=jnp.float32
    )
    return (cross_product * (1.0 / (2.0 * K))).astype(jnp.bfloat16)


def shards(strain, band_start):
    chans, windows, samp_dev = strain.shape
    flat = strain.reshape(chans * windows, samp_dev)
    band_index = lax.axis_index("band")
    bins = jnp.arange(K, dtype=jnp.int32)
    positions = band_index * samp_dev + jnp.arange(samp_dev, dtype=jnp.int32)
    own_rows = band_start.shape[0] // lax.axis_size("band")
    table = dft_table(band_start[:, None] + bins[None, :], positions)
    partial_sum = jnp.dot(
        flat,
        table.reshape(samp_dev, own_rows * lax.axis_size("band") * 2 * K),
        preferred_element_type=jnp.float32,
    )
    spectrum = lax.psum_scatter(
        partial_sum.reshape(chans * windows, own_rows * lax.axis_size("band"), 2 * K).transpose(
            1, 0, 2
        ),
        "band",
        scatter_dimension=0,
        tiled=True,
    )[0]
    panel = whiten(spectrum, chans, windows)
    result = cross_block(panel, lax.all_gather(panel, "chan", axis=0, tiled=True))
    return result[None]


def solution(mesh):
    return jax.shard_map(
        shards,
        mesh=mesh,
        in_specs=(P("chan", None, "band"), P()),
        out_specs=P("band", None, "chan", None),
        check_vma=False,
    )
```

profile of v0, /device:TPU:0, one launch (start us, length us, event | category | flops | bytes accessed | tf_op | source)
XLA Modules:
  0.0 110.6 jit_solution(17581041792112892675)
XLA Ops:
  6.5 0.0 reduce-scatter.2.cloned.1.call-start
  6.5 0.1 multiply_subtract_fusion
  6.6 0.7 iota_add_fusion.1
  7.3 6.9 %reshape.73 = bf16[1024,2048]{1,0:T(8,128)(2,1)} reshape(bf16[256,4,2048]{2,1,0:T(4,128)(2,1)} %param.2) | data formatting | bytes 8388608 | tf_op jit(solution)/shard_map/reshape | solution.py:40
  14.2 2.3 %multiply_convert_fusion.3 = (bf16[2048,2,32]{0,2,1:T(8,128)(2,1)S(1)}, bf16[2048,2,32]{0,2,1:T(8,128)(2,1)S(1)}) fusion(s32[2,32]{1,0:T(2,128)S(1)} %iota_add_fusion.1, s32[2048]{0:T(1024)S(1)} %iota_add_fusion, f32[2048]{0:T(1024)S(1)} %get-tuple-element.9, f32[2048]{0:T(1024)S(1)} %get-tuple-element.10), kind=kLoop, calls=%fused_computation.20 | loop fusion | flops 2359296 | bytes 549120 | tf_op jit(solution)/shard_map/convert
  16.5 3.7 %fusion.10 = f32[128,1024]{1,0:T(8,128)S(1)} fusion(bf16[2048,128]{0,1:T(8,128)(2,1)S(1)} %bitcast.22, bf16[1024,2048]{1,0:T(8,128)(2,1)} %reshape.73), kind=kOutput, calls=%fused_computation.27 | convolution fusion | flops 536870912 | bytes 5242880 | tf_op jit(solution)/shard_map/dot_general | solution.py:46
  20.2 1.3 %copy.5 = f32[1024,2,64]{2,0,1:T(8,128)} copy(f32[1024,2,64]{0,2,1:T(8,128)S(1)} %bitcast.21) | data formatting | bytes 1048576 | tf_op jit(solution)/shard_map/reshape | solution.py:52
  21.5 0.0 reduce-scatter.2.cloned.1.call-update
  21.6 0.0 all-gather.2.cloned.1.call-start
  21.6 23.2 %reduce-scatter.2.cloned.1.call-done = f32[1,1024,64]{2,1,0:T(8,128)} async-done(((f32[2,1024,64]{2,1,0:T(8,128)}), f32[1,1024,64]{2,1,0:T(8,128)}) %reduce-scatter.2.cloned.1.call-update) | async-done | bytes 262160 | tf_op jit(solution)/shard_map/reduce_scatter | solution.py:51
  44.8 1.2 %multiply_reduce_fusion = f32[1024]{0:T(1024)S(1)} fusion(f32[1,1024,64]{2,1,0:T(8,128)} %reduce-scatter.2.cloned.1.call-done), kind=kLoop, calls=%fused_computation.18 | loop fusion | flops 130048 | bytes 266240 | tf_op jit(solution)/shard_map/reduce_sum | solution.py:21
  46.1 0.1 rsqrt.12
  46.2 1.7 %squeeze.3 = f32[256,4,2,32]{3,2,1,0:T(2,128)S(1)} reshape(f32[1,1024,64]{2,1,0:T(8,128)} %reduce-scatter.2.cloned.1.call-done) | data formatting | bytes 524288 | tf_op jit(solution)/shard_map/squeeze | solution.py:51
  47.9 1.7 %fusion.7 = bf16[256,2,4,32]{3,1,2,0:T(2,128)(2,1)S(1)} fusion(f32[256,4,2,32]{3,2,1,0:T(2,128)S(1)} %squeeze.3, f32[256,4]{1,0:T(8,128)S(1)} %rsqrt.12), kind=kLoop, calls=%fused_computation.16 | loop fusion | flops 131072 | bytes 397312 | tf_op jit(solution)/shard_map/transpose | solution.py:24
  49.6 0.5 copy.6
  50.1 0.8 copy.7
  50.8 0.0 all-gather.2.cloned.1.call-update
  50.9 41.6 %all-gather.2.cloned.1.call-done = bf16[4096,256]{1,0:T(8,128)(2,1)} async-done(((bf16[256,256]{1,0:T(8,128)(2,1)}), bf16[4096,256]{1,0:T(8,128)(2,1)}) %all-gather.2.cloned.1.call-update) | async-done | bytes 2097168 | tf_op jit(solution)/shard_map/all_gather | solution.py:60
  92.5 0.0 copy-start
  92.5 1.9 %slice_negate_fusion = (bf16[4096,128]{1,0:T(8,128)(2,1)S(1)}, bf16[4096,128]{1,0:T(8,128)(2,1)S(1)}) fusion(bf16[4096,256]{1,0:T(8,128)(2,1)} %all-gather.2.cloned.1.call-done), kind=kLoop, calls=%fused_computation.6 | loop fusion | flops 524288 | bytes 4194304 | tf_op jit(solution)/shard_map/neg | solution.py:30
  94.4 0.2 maximum_bitcast_fusion
  94.6 0.1 copy-done
  94.7 2.7 %fusion = bf16[1,2,256,4096]{2,3,1,0:T(8,128)(2,1)} fusion(bf16[256,256,1]{0,1,2:T(8,128)(2,1)S(1)} %bitcast.25, bf16[1,4096,256]{2,1,0:T(8,128)(2,1)S(1)} %maximum_bitcast_fusion, bf16[1,4096,256]{2,1,0:T(8,128)(2,1)S(1)} %bitcast.23), kind=kOutput, calls=%fused_computation.1 | convolution fusion | flops 1080033280 | bytes 8519680 | tf_op jit(solution)/shard_map/gb,ozb->ogz/dot_general | solution.py:32
  97.4 6.3 %copy.9 = bf16[1,2,256,4096]{3,2,1,0:T(8,128)(2,1)} copy(bf16[1,2,256,4096]{2,3,1,0:T(8,128)(2,1)} %fusion) | data formatting | bytes 8388608 | tf_op jit(solution)/shard_map/broadcast_in_dim | solution.py:61
  (3 shorter events, 0.0 us)
Async XLA Ops:
  6.5 38.3 %reduce-scatter.2.cloned.1.call-start = ((), (), s32[]{:S(2)}) async-start(), calls=%async_computation.1 | async-start | bytes 1572864 | tf_op jit(solution)/shard_map/reduce_scatter | solution.py:51
  21.6 70.9 %all-gather.2.cloned.1.call-start = ((), (), s32[]{:S(2)}) async-start(), calls=%async_computation.2 | async-start | bytes 2228224 | tf_op jit(solution)/shard_map/all_gather | solution.py:60
  92.5 2.2 %copy-start = (bf16[4096,256]{1,0:T(8,128)(2,1)S(1)}, bf16[4096,256]{1,0:T(8,128)(2,1)}, u32[]{:S(2)}) copy-start(bf16[4096,256]{1,0:T(8,128)(2,1)} %all-gather.2.cloned.1.call-done) | copy-start | bytes 6291460
Sparse Core Ops, SparseCore 0:
  21.7 23.0 reduce-scatter.1
  51.0 41.4 all-gather.1
where the time goes:
time: 111 us
  waiting for transfers between devices  64.9 us (58%)
  local copies, waits for them, and re-layouts  17.6 us (16%)
  between operations  13.5 us (12%)
  other arithmetic  8.16 us (7%)
  matrix products  6.46 us (6%)
    all_gather x1, waiting for transfers between devices, shards(): lax.all_gather(panel, 'chan', axis=0, tiled=True)  41.6 us
    reduce_scatter x1, waiting for transfers between devices, shards(): lax.psum_scatter(partial_sum.reshape(chans * windows, own_rows * lax.axis...  23.2 us
    reshape x1, local copies, waits for them, and re-layouts, shards(): flat = strain.reshape(chans * windows, samp_dev)  6.86 us
    broadcast_in_dim x1, local copies, waits for them, and re-layouts, shards(): return result[None]  6.31 us
    dot_general x1, matrix products, shards(): jnp.dot(flat, table.reshape(samp_dev, own_rows * lax.axis_size('band') *...  3.73 us
    dot_general x1, matrix products, cross_block(): jnp.einsum('gb,ozb->ogz', local_panel_rows, stacked_spectra, preferred_el...  2.73 us
    another operation x1, other arithmetic  2.25 us
  transfers between devices with their start and end apart: 2, of which 2 were waited for; matrix products, arithmetic and copies ran while one was open for 0% of the time, Pallas kernels for 0%

commit v1 on v0

--- a/solution.py
+++ b/solution.py
@@ -57,7 +57,12 @@
         tiled=True,
     )[0]
     panel = whiten(spectrum, chans, windows)
-    result = cross_block(panel, lax.all_gather(panel, "chan", axis=0, tiled=True))
+    result = cross_block(
+        panel,
+        jnp.concatenate(
+            lax.all_to_all(jnp.stack([panel] * lax.axis_size("chan")), "chan", 0, 0), axis=0
+        ),
+    )
     return result[None]
 
 

time: 111 us -> 120 us (1.081)
  blocking collectives: 0 us -> 52.6 us
  waiting for transfers between devices: 64.9 us -> 23.3 us
  other arithmetic: 8.16 us -> 6.52 us
    all_to_all x0 -> x1, blocking collectives: none -> 52.6 us  [shards(): lax.all_to_all(jnp.stack([panel] * lax.axis_size('chan')), 'chan', 0, 0)]
    all_gather x1 -> x0, waiting for transfers between devices: 41.6 us -> none  [shards(): lax.all_gather(panel, 'chan', axis=0, tiled=True)]
    neg x1, other arithmetic: 1.89 us -> 0.25 us  [cross_block(): -other_panel[:, half_feat:]]
  transfers between devices with their start and end apart: 2 -> 1, of which waited for: 2 -> 1; matrix products, arithmetic and copies ran while one was open for 0% -> 0% of each run, Pallas kernels for 0% -> 0%
where the time goes in v1:
time: 120 us; the launch traced here: 119 us
  blocking collectives  52.6 us (44%)
  waiting for transfers between devices  23.3 us (19%)
  local copies, waits for them, and re-layouts  17 us (14%)
  between operations  13.5 us (11%)
  other arithmetic  6.52 us (5%)
  matrix products  6.48 us (5%)
    all_to_all x1, blocking collectives, shards(): lax.all_to_all(jnp.stack([panel] * lax.axis_size('chan')), 'chan', 0, 0)  52.6 us
    reduce_scatter x1, waiting for transfers between devices, shards(): lax.psum_scatter(partial_sum.reshape(chans * windows, own_rows * lax.axis...  23.3 us
    reshape x1, local copies, waits for them, and re-layouts, shards(): flat = strain.reshape(chans * windows, samp_dev)  6.86 us
    broadcast_in_dim x1, local copies, waits for them, and re-layouts, shards(): return result[None]  6.31 us
    dot_general x1, matrix products, shards(): jnp.dot(flat, table.reshape(samp_dev, own_rows * lax.axis_size('band') *...  3.73 us
    dot_general x1, matrix products, cross_block(): jnp.einsum('gb,ozb->ogz', local_panel_rows, stacked_spectra, preferred_el...  2.75 us
  transfers between devices with their start and end apart: 1, of which 1 were waited for; matrix products, arithmetic and copies ran while one was open for 0% of the time, Pallas kernels for 0%

profile of v1, /device:TPU:0, one launch (start us, length us, event | category | flops | bytes accessed | tf_op | source)
XLA Modules:
  0.0 119.4 jit_solution(9734976644240853414)
XLA Ops:
  6.5 0.0 reduce-scatter.2.cloned.1.call-start
  6.5 0.1 multiply_subtract_fusion
  6.6 0.7 iota_add_fusion.1
  7.3 6.9 %reshape.76 = bf16[1024,2048]{1,0:T(8,128)(2,1)} reshape(bf16[256,4,2048]{2,1,0:T(4,128)(2,1)} %param.2) | data formatting | bytes 8388608 | tf_op jit(solution)/shard_map/reshape | solution.py:40
  14.2 2.3 %multiply_convert_fusion.3 = (bf16[2048,2,32]{0,2,1:T(8,128)(2,1)S(1)}, bf16[2048,2,32]{0,2,1:T(8,128)(2,1)S(1)}) fusion(s32[2,32]{1,0:T(2,128)S(1)} %iota_add_fusion.1, s32[2048]{0:T(1024)S(1)} %iota_add_fusion, f32[2048]{0:T(1024)S(1)} %get-tuple-element.9, f32[2048]{0:T(1024)S(1)} %get-tuple-element.10), kind=kLoop, calls=%fused_computation.20 | loop fusion | flops 2359296 | bytes 549120 | tf_op jit(solution)/shard_map/convert
  16.5 3.7 %fusion.10 = f32[128,1024]{1,0:T(8,128)S(1)} fusion(bf16[2048,128]{0,1:T(8,128)(2,1)S(1)} %bitcast.25, bf16[1024,2048]{1,0:T(8,128)(2,1)} %reshape.76), kind=kOutput, calls=%fused_computation.27 | convolution fusion | flops 536870912 | bytes 5242880 | tf_op jit(solution)/shard_map/dot_general | solution.py:46
  20.2 1.3 %copy.5 = f32[1024,2,64]{2,0,1:T(8,128)} copy(f32[1024,2,64]{0,2,1:T(8,128)S(1)} %bitcast.24) | data formatting | bytes 1048576 | tf_op jit(solution)/shard_map/reshape | solution.py:52
  21.5 0.0 reduce-scatter.2.cloned.1.call-update
  21.6 23.3 %reduce-scatter.2.cloned.1.call-done = f32[1,1024,64]{2,1,0:T(8,128)} async-done(((f32[2,1024,64]{2,1,0:T(8,128)}), f32[1,1024,64]{2,1,0:T(8,128)}) %reduce-scatter.2.cloned.1.call-update) | async-done | bytes 262160 | tf_op jit(solution)/shard_map/reduce_scatter | solution.py:51
  44.8 1.2 %multiply_reduce_fusion = f32[1024]{0:T(1024)S(1)} fusion(f32[1,1024,64]{2,1,0:T(8,128)} %reduce-scatter.2.cloned.1.call-done), kind=kLoop, calls=%fused_computation.18 | loop fusion | flops 130048 | bytes 266240 | tf_op jit(solution)/shard_map/reduce_sum | solution.py:21
  46.1 0.1 rsqrt.12
  46.2 1.7 %squeeze.3 = f32[256,4,2,32]{3,2,1,0:T(2,128)S(1)} reshape(f32[1,1024,64]{2,1,0:T(8,128)} %reduce-scatter.2.cloned.1.call-done) | data formatting | bytes 524288 | tf_op jit(solution)/shard_map/squeeze | solution.py:51
  47.9 1.7 %fusion.7 = bf16[256,2,4,32]{3,1,2,0:T(2,128)(2,1)S(1)} fusion(f32[256,4,2,32]{3,2,1,0:T(2,128)S(1)} %squeeze.3, f32[256,4]{1,0:T(8,128)S(1)} %rsqrt.12), kind=kLoop, calls=%fused_computation.16 | loop fusion | flops 131072 | bytes 397312 | tf_op jit(solution)/shard_map/transpose | solution.py:24
  49.6 0.5 copy.6
  50.1 0.1 copy.7
  50.2 0.2 stack.9
  50.4 52.6 %all_to_all.5 = bf16[16,256,256]{2,1,0:T(8,128)(2,1)S(1)} all-to-all(bf16[16,256,256]{2,1,0:T(8,128)(2,1)S(1)} %stack.9), channel_id=1, replica_groups=mesh['chan'=16,'band'=2] {'chan'}, dimensions={0} | all-to-all | bytes 4194304 | tf_op jit(solution)/shard_map/all_to_all | solution.py:63
  103.0 0.2 slice_negate_fusion
  103.2 0.2 maximum_bitcast_fusion
  103.5 2.8 %fusion = bf16[1,2,256,4096]{2,3,1,0:T(8,128)(2,1)} fusion(bf16[256,256,1]{0,1,2:T(8,128)(2,1)S(1)} %bitcast.27, bf16[1,4096,256]{2,1,0:T(8,128)(2,1)S(1)} %maximum_bitcast_fusion, bf16[1,4096,256]{2,1,0:T(8,128)(2,1)S(1)} %bitcast.22), kind=kOutput, calls=%fused_computation.1 | convolution fusion | flops 1080033280 | bytes 8519680 | tf_op jit(solution)/shard_map/gb,ozb->ogz/dot_general | solution.py:32
  106.2 6.3 %copy.9 = bf16[1,2,256,4096]{3,2,1,0:T(8,128)(2,1)} copy(bf16[1,2,256,4096]{2,3,1,0:T(8,128)(2,1)} %fusion) | data formatting | bytes 8388608 | tf_op jit(solution)/shard_map/broadcast_in_dim | solution.py:66
  (3 shorter events, 0.0 us)
Async XLA Ops:
  6.5 38.3 %reduce-scatter.2.cloned.1.call-start = ((), (), s32[]{:S(2)}) async-start(), calls=%async_computation.2 | async-start | bytes 1572864 | tf_op jit(solution)/shard_map/reduce_scatter | solution.py:51
Sparse Core Ops, SparseCore 0:
  21.7 23.0 reduce-scatter.1
